TPU v7x, 512 devices: a whole 4x8x8 slice. The times are simulated.
512 devices in a mesh: mem: 16 (over y, core), lat: 8 (over x, z_hi), lon: 4 (over z_lo).
Axes of the slice: x: 4, y: 8, z: 8 (z_hi: 2, z_lo: 4; z = z_hi * 4 + z_lo), core: 2. Of those that a mesh axis runs over, the one named last changes fastest.
Arguments:
- members: bfloat16 [32, 8, 256, 512], P('mem', None, 'lat', 'lon'), may hold values from -6 to 6
- increment: float32 [8, 256, 512], P(None, 'lat', 'lon'), may hold values from -6 to 6
Outputs:
- covariance_product: float32 [8, 256, 512], P(None, 'lat', 'lon')
All inputs are finite; a program needn't handle non-finite values.
Results may differ from a plain program's by a relative error of at most 0.0003.
Values sent between devices are 32-bit elements; how exact they have to be, the bound alone decides.
No kernel may reach another device: no remote copies, remote signals or barrier semaphores. Data moves between devices by JAX's collectives and lax.ppermute only.
A program may use at most 64 MiB of HBM per device.

v0:
```python
import jax
import jax.numpy as jnp
from jax import lax
from jax.sharding import PartitionSpec as P

ITERS = 4
factors = (1, 2, 4)
stiffnesses = (1.0, 2.0, 4.0)
weights = (0.5, 0.3, 0.2)


def with_halo(block, sides, width, periodic):
    for axis, dim in sides:
        count = lax.axis_size(axis)
        forward = [(i, i + 1) for i in range(count - 1)]
        if periodic:
            forward.append((count - 1, 0))
        backward = [(target, source) for source, target in forward]
        low = lax.ppermute(
            lax.slice_in_dim(block, block.shape[dim] - width, None, axis=dim), axis, forward
        )
        high = lax.ppermute(lax.slice_in_dim(block, 0, width, axis=dim), axis, backward)
        block = jnp.concatenate([low, block, high], axis=dim)
    return block


def coarsen(values_now, factor):
    if factor == 1:
        return values_now
    dims_now = values_now.shape
    blocks = values_now.reshape(
        dims_now[:-2] + (dims_now[-2] // factor, factor, dims_now[-1] // factor, factor)
    )
    return jnp.mean(blocks, axis=(-3, -1))


def refine(values_now, factor):
    if factor == 1:
        return values_now
    return jnp.repeat(jnp.repeat(values_now, factor, axis=-2), factor, axis=-1)


def diffuse_single(source, stiffness):
    smoothed = source
    for sweeps in range(ITERS):
        with_rows = with_halo(smoothed, (("lat", 2),), 1, False)
        with_cols = with_halo(smoothed, (("lon", 3),), 1, True)
        beside_all = with_rows[:, :, :-2, :] + with_rows[:, :, 2:, :]
        beside_all = beside_all + with_cols[:, :, :, :-2] + with_cols[:, :, :, 2:]
        smoothed = (source + stiffness * beside_all) / (1.0 + 4.0 * stiffness)
    return smoothed


def body(members, increment):
    member_field = members.astype(jnp.float32)
    product = member_field * increment[None]
    running = jnp.zeros(member_field.shape, jnp.float32)
    for factor, stiffness, weight in zip(factors, stiffnesses, weights):
        source = coarsen(product, factor)
        coarse = diffuse_single(source, stiffness)
        running = running + weight * member_field * refine(coarse, factor)
    partial_value = jnp.sum(running, axis=0)
    member_count = members.shape[0] * lax.axis_size("mem")
    summed = lax.psum(partial_value, "mem")
    return summed / (member_count - 1)


def solution(mesh):
    return jax.shard_map(
        body,
        mesh=mesh,
        in_specs=(P("mem", None, "lat", "lon"), P(None, "lat", "lon")),
        out_specs=P(None, "lat", "lon"),
        check_vma=False,
    )
```

profile of v0, /device:TPU:1, one launch (start us, length us, event | category | flops | bytes accessed | tf_op | source)
XLA Modules:
  0.0 434.9 jit_solution(4924736812012016826)
XLA Ops:
  9.0 4.3 copy.364
  13.3 5.6 %reduce_sum.27 = f32[2,8,16,64]{1,3,2,0:T(8,128)S(1)} reduce(f32[2,8,16,2,64,2]{1,5,4,3,2,0:T(2,128)} %bitcast.6, f32[]{:T(128)} %constant.30.clone.1), dimensions={3,5}, to_apply=%region_0.0 | reduce | flops 49152 | bytes 327684 | tf_op jit(solution)/shard_map/reduce_sum | solution.py:34
  20.1 8.4 %collective-permute-start.19 = (f32[2,8,16,1]{3,2,1,0:T(8,128)}, f32[2,8,16,1]{3,2,1,0:T(8,128)}, u32[]{:S(2)}, u32[]{:S(2)}) collective-permute-start(f32[2,8,16,1]{3,2,1,0:T(8,128)} %get-tuple-element.52), channel_id=1, source_target_pairs={{1,0},{2,1},{3,2},{0,3},{5,4},{6,5},{7,6},{4,7},{9,8},{10,9},{11,1... | collective-permute-start | bytes 3080 | tf_op jit(solution)/shard_map/ppermute | solution.py:22
  28.5 3.6 reduce_sum.28
  34.1 3.4 collective-permute-start.34
  38.8 8.6 %collective-permute-start.32 = (f32[2,8,1,32]{1,3,2,0:T(8,128)S(1)}, f32[2,8,1,32]{1,3,2,0:T(8,128)S(1)}, u32[]{:S(2)}, u32[]{:S(2)}) collective-permute-start(f32[2,8,1,32]{1,3,2,0:T(8,128)S(1)} %get-tuple-element.33), channel_id=1, source_target_pairs={{0,4},{4,8},{8,12},{12,16},{16,20},{20,24},{24,28},{1,5},{5,9},{9,... | collective-permute-start | bytes 6152 | tf_op jit(solution)/shard_map/ppermute | solution.py:19
  51.7 4.0 collective-permute-start.39
  58.9 9.4 %collective-permute-start.36 = (f32[2,8,1,32]{1,3,2,0:T(8,128)}, f32[2,8,1,32]{1,3,2,0:T(8,128)}, u32[]{:S(2)}, u32[]{:S(2)}) collective-permute-start(f32[2,8,1,32]{1,3,2,0:T(8,128)} %get-tuple-element.29), channel_id=1, source_target_pairs={{0,4},{4,8},{8,12},{12,16},{16,20},{20,24},{24,28},{1,5},{5,9},{9,... | collective-permute-start | bytes 6152 | tf_op jit(solution)/shard_map/ppermute | solution.py:19
  74.6 8.2 %collective-permute-start.16 = (f32[2,8,1,64]{3,2,1,0:T(1,128)}, f32[2,8,1,64]{3,2,1,0:T(1,128)S(1)}, u32[]{:S(2)}, u32[]{:S(2)}) collective-permute-start(f32[2,8,1,64]{3,2,1,0:T(1,128)} %get-tuple-element.49), channel_id=1, source_target_pairs={{0,4},{4,8},{8,12},{12,16},{16,20},{20,24},{24,28},{1,5},{5,9},{9,... | collective-permute-start | bytes 12296 | tf_op jit(solution)/shard_map/ppermute | solution.py:19
  82.9 5.2 %collective-permute-start.3 = (f32[2,8,32,1]{2,1,3,0:T(8,128)}, f32[2,8,32,1]{2,1,3,0:T(8,128)S(1)}, u32[]{:S(2)}, u32[]{:S(2)}) collective-permute-start(f32[2,8,32,1]{2,1,3,0:T(8,128)} %get-tuple-element.20), channel_id=1, source_target_pairs={{1,0},{2,1},{3,2},{0,3},{5,4},{6,5},{7,6},{4,7},{9,8},{10,9},{11,1... | collective-permute-start | bytes 6152 | tf_op jit(solution)/shard_map/ppermute | solution.py:22
  91.2 3.4 collective-permute-start.43
  97.8 8.8 %collective-permute-start.40 = (f32[2,8,1,32]{1,3,2,0:T(8,128)S(1)}, f32[2,8,1,32]{1,3,2,0:T(8,128)S(1)}, u32[]{:S(2)}, u32[]{:S(2)}) collective-permute-start(f32[2,8,1,32]{1,3,2,0:T(8,128)S(1)} %get-tuple-element.25), channel_id=1, source_target_pairs={{0,4},{4,8},{8,12},{12,16},{16,20},{20,24},{24,28},{1,5},{5,9},{9,... | collective-permute-start | bytes 6152 | tf_op jit(solution)/shard_map/ppermute | solution.py:19
  106.6 5.2 %collective-permute-start.23 = (f32[2,8,16,1]{3,2,1,0:T(8,128)S(1)}, f32[2,8,16,1]{3,2,1,0:T(8,128)S(1)}, u32[]{:S(2)}, u32[]{:S(2)}) collective-permute-start(f32[2,8,16,1]{3,2,1,0:T(8,128)S(1)} %get-tuple-element.48), channel_id=1, source_target_pairs={{1,0},{2,1},{3,2},{0,3},{5,4},{6,5},{7,6},{4,7},{9,8},{10,9},{11,1... | collective-permute-start | bytes 3080 | tf_op jit(solution)/shard_map/ppermute | solution.py:22
  115.1 8.8 %collective-permute-start.20 = (f32[2,8,1,64]{3,2,1,0:T(1,128)S(1)}, f32[2,8,1,64]{3,2,1,0:T(1,128)S(1)}, u32[]{:S(2)}, u32[]{:S(2)}) collective-permute-start(f32[2,8,1,64]{3,2,1,0:T(1,128)S(1)} %get-tuple-element.45), channel_id=1, source_target_pairs={{0,4},{4,8},{8,12},{12,16},{16,20},{20,24},{24,28},{1,5},{5,9},{9,... | collective-permute-start | bytes 12296 | tf_op jit(solution)/shard_map/ppermute | solution.py:19
  128.6 8.8 %collective-permute-start = (f32[2,8,1,128]{3,1,2,0:T(8,128)S(1)}, f32[2,8,1,128]{3,1,2,0:T(8,128)S(1)}, u32[]{:S(2)}, u32[]{:S(2)}) collective-permute-start(f32[2,8,1,128]{3,1,2,0:T(8,128)S(1)} %copy.348), channel_id=1, source_target_pairs={{0,4},{4,8},{8,12},{12,16},{16,20},{20,24},{24,28},{1,5},{5,9},{9,... | collective-permute-start | bytes 24584 | tf_op jit(solution)/shard_map/ppermute | solution.py:19
  137.4 5.2 %collective-permute-start.47 = (f32[2,8,8,1]{1,3,2,0:T(1,128)}, f32[2,8,8,1]{1,3,2,0:T(1,128)}, u32[]{:S(2)}, u32[]{:S(2)}) collective-permute-start(f32[2,8,8,1]{1,3,2,0:T(1,128)} %get-tuple-element.24), channel_id=1, source_target_pairs={{1,0},{2,1},{3,2},{0,3},{5,4},{6,5},{7,6},{4,7},{9,8},{10,9},{11,1... | collective-permute-start | bytes 1544 | tf_op jit(solution)/shard_map/ppermute | solution.py:22
  149.5 8.8 %collective-permute-start.44 = (f32[2,8,1,32]{1,3,2,0:T(8,128)}, f32[2,8,1,32]{1,3,2,0:T(8,128)S(1)}, u32[]{:S(2)}, u32[]{:S(2)}) collective-permute-start(f32[2,8,1,32]{1,3,2,0:T(8,128)} %get-tuple-element.21), channel_id=1, source_target_pairs={{0,4},{4,8},{8,12},{12,16},{16,20},{20,24},{24,28},{1,5},{5,9},{9,... | collective-permute-start | bytes 6152 | tf_op jit(solution)/shard_map/ppermute | solution.py:19
  158.9 5.3 %collective-permute-start.27 = (f32[2,8,16,1]{3,2,1,0:T(8,128)}, f32[2,8,16,1]{3,2,1,0:T(8,128)}, u32[]{:S(2)}, u32[]{:S(2)}) collective-permute-start(f32[2,8,16,1]{3,2,1,0:T(8,128)} %get-tuple-element.44), channel_id=1, source_target_pairs={{1,0},{2,1},{3,2},{0,3},{5,4},{6,5},{7,6},{4,7},{9,8},{10,9},{11,1... | collective-permute-start | bytes 3080 | tf_op jit(solution)/shard_map/ppermute | solution.py:22
  164.2 2.5 fusion.23
  172.8 9.4 %collective-permute-start.24 = (f32[2,8,1,64]{3,2,1,0:T(1,128)}, f32[2,8,1,64]{3,2,1,0:T(1,128)}, u32[]{:S(2)}, u32[]{:S(2)}) collective-permute-start(f32[2,8,1,64]{3,2,1,0:T(1,128)} %get-tuple-element.41), channel_id=1, source_target_pairs={{0,4},{4,8},{8,12},{12,16},{16,20},{20,24},{24,28},{1,5},{5,9},{9,... | collective-permute-start | bytes 12296 | tf_op jit(solution)/shard_map/ppermute | solution.py:19
  187.8 5.1 %collective-permute-start.7 = (f32[2,8,32,1]{2,1,3,0:T(8,128)}, f32[2,8,32,1]{2,1,3,0:T(8,128)S(1)}, u32[]{:S(2)}, u32[]{:S(2)}) collective-permute-start(f32[2,8,32,1]{2,1,3,0:T(8,128)} %get-tuple-element.16), channel_id=1, source_target_pairs={{1,0},{2,1},{3,2},{0,3},{5,4},{6,5},{7,6},{4,7},{9,8},{10,9},{11,1... | collective-permute-start | bytes 6152 | tf_op jit(solution)/shard_map/ppermute | solution.py:22
  199.3 8.2 %collective-permute-start.4 = (f32[2,8,1,128]{3,1,2,0:T(8,128)}, f32[2,8,1,128]{3,1,2,0:T(8,128)S(1)}, u32[]{:S(2)}, u32[]{:S(2)}) collective-permute-start(f32[2,8,1,128]{3,1,2,0:T(8,128)} %copy.352), channel_id=1, source_target_pairs={{0,4},{4,8},{8,12},{12,16},{16,20},{20,24},{24,28},{1,5},{5,9},{9,... | collective-permute-start | bytes 24584 | tf_op jit(solution)/shard_map/ppermute | solution.py:19
  212.4 2.4 fusion.18
  216.8 5.1 %collective-permute-start.11 = (f32[2,8,32,1]{2,1,3,0:T(8,128)}, f32[2,8,32,1]{2,1,3,0:T(8,128)S(1)}, u32[]{:S(2)}, u32[]{:S(2)}) collective-permute-start(f32[2,8,32,1]{2,1,3,0:T(8,128)} %get-tuple-element.12), channel_id=1, source_target_pairs={{1,0},{2,1},{3,2},{0,3},{5,4},{6,5},{7,6},{4,7},{9,8},{10,9},{11,1... | collective-permute-start | bytes 6152 | tf_op jit(solution)/shard_map/ppermute | solution.py:22
  228.3 8.8 %collective-permute-start.8 = (f32[2,8,1,128]{3,1,2,0:T(8,128)}, f32[2,8,1,128]{3,1,2,0:T(8,128)S(1)}, u32[]{:S(2)}, u32[]{:S(2)}) collective-permute-start(f32[2,8,1,128]{3,1,2,0:T(8,128)} %copy.356), channel_id=1, source_target_pairs={{0,4},{4,8},{8,12},{12,16},{16,20},{20,24},{24,28},{1,5},{5,9},{9,... | collective-permute-start | bytes 24584 | tf_op jit(solution)/shard_map/ppermute | solution.py:19
  237.7 5.2 %collective-permute-start.31 = (f32[2,8,16,1]{3,2,1,0:T(8,128)}, f32[2,8,16,1]{3,2,1,0:T(8,128)}, u32[]{:S(2)}, u32[]{:S(2)}) collective-permute-start(f32[2,8,16,1]{3,2,1,0:T(8,128)} %get-tuple-element.40), channel_id=1, source_target_pairs={{1,0},{2,1},{3,2},{0,3},{5,4},{6,5},{7,6},{4,7},{9,8},{10,9},{11,1... | collective-permute-start | bytes 3080 | tf_op jit(solution)/shard_map/ppermute | solution.py:22
  248.9 9.4 %collective-permute-start.28 = (f32[2,8,1,64]{3,2,1,0:T(1,128)}, f32[2,8,1,64]{3,2,1,0:T(1,128)}, u32[]{:S(2)}, u32[]{:S(2)}) collective-permute-start(f32[2,8,1,64]{3,2,1,0:T(1,128)} %get-tuple-element.37), channel_id=1, source_target_pairs={{0,4},{4,8},{8,12},{12,16},{16,20},{20,24},{24,28},{1,5},{5,9},{9,... | collective-permute-start | bytes 12296 | tf_op jit(solution)/shard_map/ppermute | solution.py:19
  258.3 2.4 fusion.13
  262.7 5.1 %collective-permute-start.15 = (f32[2,8,32,1]{2,1,3,0:T(8,128)}, f32[2,8,32,1]{2,1,3,0:T(8,128)S(1)}, u32[]{:S(2)}, u32[]{:S(2)}) collective-permute-start(f32[2,8,32,1]{2,1,3,0:T(8,128)} %get-tuple-element.8), channel_id=1, source_target_pairs={{1,0},{2,1},{3,2},{0,3},{5,4},{6,5},{7,6},{4,7},{9,8},{10,9},{11,1... | collective-permute-start | bytes 6152 | tf_op jit(solution)/shard_map/ppermute | solution.py:22
  274.2 8.8 %collective-permute-start.12 = (f32[2,8,1,128]{3,1,2,0:T(8,128)}, f32[2,8,1,128]{3,1,2,0:T(8,128)}, u32[]{:S(2)}, u32[]{:S(2)}) collective-permute-start(f32[2,8,1,128]{3,1,2,0:T(8,128)} %copy.360), channel_id=1, source_target_pairs={{0,4},{4,8},{8,12},{12,16},{16,20},{20,24},{24,28},{1,5},{5,9},{9,... | collective-permute-start | bytes 24584 | tf_op jit(solution)/shard_map/ppermute | solution.py:19
  289.6 3.2 fusion.3
  294.7 131.7 %all-reduce.2.cloned.1.call-done = f32[8,32,128]{2,1,0:T(8,128)} async-done(((f32[8,32,128]{2,1,0:T(8,128)}), f32[8,32,128]{2,1,0:T(8,128)}) %all-reduce.2.cloned.1.call-update) | async-done | bytes 131088 | tf_op jit(solution)/shard_map/psum | solution.py:64
  (154 shorter events, 98.4 us)
Async XLA Ops:
  6.5 419.9 %all-reduce.2.cloned.1.call-start = ((), (), s32[]{:S(2)}) async-start(), calls=%async_computation | async-start | bytes 262144 | tf_op jit(solution)/shard_map/psum | solution.py:64
  20.1 69.4 %collective-permute-start.19 = (f32[2,8,16,1]{3,2,1,0:T(8,128)}, f32[2,8,16,1]{3,2,1,0:T(8,128)}, u32[]{:S(2)}, u32[]{:S(2)}) collective-permute-start(f32[2,8,16,1]{3,2,1,0:T(8,128)} %get-tuple-element.52), channel_id=1, source_target_pairs={{1,0},{2,1},{3,2},{0,3},{5,4},{6,5},{7,6},{4,7},{9,8},{10,9},{11,1... | collective-permute-start | bytes 3080 | tf_op jit(solution)/shard_map/ppermute | solution.py:22
  32.2 18.0 %collective-permute-start.35 = (f32[2,8,8,1]{1,3,2,0:T(1,128)S(1)}, f32[2,8,8,1]{1,3,2,0:T(1,128)S(1)}, u32[]{:S(2)}, u32[]{:S(2)}) collective-permute-start(f32[2,8,8,1]{1,3,2,0:T(1,128)S(1)} %get-tuple-element.36), channel_id=1, source_target_pairs={{1,0},{2,1},{3,2},{0,3},{5,4},{6,5},{7,6},{4,7},{9,8},{10,9},{11,1... | collective-permute-start | bytes 1544 | tf_op jit(solution)/shard_map/ppermute | solution.py:22
  51.7 19.7 %collective-permute-start.39 = (f32[2,8,8,1]{1,3,2,0:T(1,128)}, f32[2,8,8,1]{1,3,2,0:T(1,128)S(1)}, u32[]{:S(2)}, u32[]{:S(2)}) collective-permute-start(f32[2,8,8,1]{1,3,2,0:T(1,128)} %get-tuple-element.32), channel_id=1, source_target_pairs={{1,0},{2,1},{3,2},{0,3},{5,4},{6,5},{7,6},{4,7},{9,8},{10,9},{11,1... | collective-permute-start | bytes 1544 | tf_op jit(solution)/shard_map/ppermute | solution.py:22
  55.6 17.7 %collective-permute-start.38 = (f32[2,8,8,1]{1,3,2,0:T(1,128)}, f32[2,8,8,1]{1,3,2,0:T(1,128)}, u32[]{:S(2)}, u32[]{:S(2)}) collective-permute-start(f32[2,8,8,1]{1,3,2,0:T(1,128)} %get-tuple-element.31), channel_id=1, source_target_pairs={{0,1},{1,2},{2,3},{3,0},{4,5},{5,6},{6,7},{7,4},{8,9},{9,10},{10,1... | collective-permute-start | bytes 1544 | tf_op jit(solution)/shard_map/ppermute | solution.py:19
  58.9 24.0 %collective-permute-start.36 = (f32[2,8,1,32]{1,3,2,0:T(8,128)}, f32[2,8,1,32]{1,3,2,0:T(8,128)}, u32[]{:S(2)}, u32[]{:S(2)}) collective-permute-start(f32[2,8,1,32]{1,3,2,0:T(8,128)} %get-tuple-element.29), channel_id=1, source_target_pairs={{0,4},{4,8},{8,12},{12,16},{16,20},{20,24},{24,28},{1,5},{5,9},{9,... | collective-permute-start | bytes 6152 | tf_op jit(solution)/shard_map/ppermute | solution.py:19
  71.4 18.1 %collective-permute-start.18 = (f32[2,8,16,1]{3,2,1,0:T(8,128)}, f32[2,8,16,1]{3,2,1,0:T(8,128)S(1)}, u32[]{:S(2)}, u32[]{:S(2)}) collective-permute-start(f32[2,8,16,1]{3,2,1,0:T(8,128)} %get-tuple-element.51), channel_id=1, source_target_pairs={{0,1},{1,2},{2,3},{3,0},{4,5},{5,6},{6,7},{7,4},{8,9},{9,10},{10,1... | collective-permute-start | bytes 3080 | tf_op jit(solution)/shard_map/ppermute | solution.py:19
  82.9 66.6 %collective-permute-start.3 = (f32[2,8,32,1]{2,1,3,0:T(8,128)}, f32[2,8,32,1]{2,1,3,0:T(8,128)S(1)}, u32[]{:S(2)}, u32[]{:S(2)}) collective-permute-start(f32[2,8,32,1]{2,1,3,0:T(8,128)} %get-tuple-element.20), channel_id=1, source_target_pairs={{1,0},{2,1},{3,2},{0,3},{5,4},{6,5},{7,6},{4,7},{9,8},{10,9},{11,1... | collective-permute-start | bytes 6152 | tf_op jit(solution)/shard_map/ppermute | solution.py:22
  96.5 17.2 %collective-permute-start.41 = (f32[2,8,1,32]{1,3,2,0:T(8,128)S(1)}, f32[2,8,1,32]{1,3,2,0:T(8,128)S(1)}, u32[]{:S(2)}, u32[]{:S(2)}) collective-permute-start(f32[2,8,1,32]{1,3,2,0:T(8,128)S(1)} %get-tuple-element.26), channel_id=1, source_target_pairs={{4,0},{8,4},{12,8},{16,12},{20,16},{24,20},{28,24},{5,1},{9,5},{13... | collective-permute-start | bytes 6152 | tf_op jit(solution)/shard_map/ppermute | solution.py:22
  97.8 17.3 %collective-permute-start.40 = (f32[2,8,1,32]{1,3,2,0:T(8,128)S(1)}, f32[2,8,1,32]{1,3,2,0:T(8,128)S(1)}, u32[]{:S(2)}, u32[]{:S(2)}) collective-permute-start(f32[2,8,1,32]{1,3,2,0:T(8,128)S(1)} %get-tuple-element.25), channel_id=1, source_target_pairs={{0,4},{4,8},{8,12},{12,16},{16,20},{20,24},{24,28},{1,5},{5,9},{9,... | collective-permute-start | bytes 6152 | tf_op jit(solution)/shard_map/ppermute | solution.py:19
  106.6 18.7 %collective-permute-start.23 = (f32[2,8,16,1]{3,2,1,0:T(8,128)S(1)}, f32[2,8,16,1]{3,2,1,0:T(8,128)S(1)}, u32[]{:S(2)}, u32[]{:S(2)}) collective-permute-start(f32[2,8,16,1]{3,2,1,0:T(8,128)S(1)} %get-tuple-element.48), channel_id=1, source_target_pairs={{1,0},{2,1},{3,2},{0,3},{5,4},{6,5},{7,6},{4,7},{9,8},{10,9},{11,1... | collective-permute-start | bytes 3080 | tf_op jit(solution)/shard_map/ppermute | solution.py:22
  115.1 22.3 %collective-permute-start.20 = (f32[2,8,1,64]{3,2,1,0:T(1,128)S(1)}, f32[2,8,1,64]{3,2,1,0:T(1,128)S(1)}, u32[]{:S(2)}, u32[]{:S(2)}) collective-permute-start(f32[2,8,1,64]{3,2,1,0:T(1,128)S(1)} %get-tuple-element.45), channel_id=1, source_target_pairs={{0,4},{4,8},{8,12},{12,16},{16,20},{20,24},{24,28},{1,5},{5,9},{9,... | collective-permute-start | bytes 12296 | tf_op jit(solution)/shard_map/ppermute | solution.py:19
  125.3 33.0 %collective-permute-start.2 = (f32[2,8,32,1]{2,1,3,0:T(8,128)}, f32[2,8,32,1]{2,1,3,0:T(8,128)S(1)}, u32[]{:S(2)}, u32[]{:S(2)}) collective-permute-start(f32[2,8,32,1]{2,1,3,0:T(8,128)} %get-tuple-element.19), channel_id=1, source_target_pairs={{0,1},{1,2},{2,3},{3,0},{4,5},{5,6},{6,7},{7,4},{8,9},{9,10},{10,1... | collective-permute-start | bytes 6152 | tf_op jit(solution)/shard_map/ppermute | solution.py:19
  128.6 18.3 %collective-permute-start = (f32[2,8,1,128]{3,1,2,0:T(8,128)S(1)}, f32[2,8,1,128]{3,1,2,0:T(8,128)S(1)}, u32[]{:S(2)}, u32[]{:S(2)}) collective-permute-start(f32[2,8,1,128]{3,1,2,0:T(8,128)S(1)} %copy.348), channel_id=1, source_target_pairs={{0,4},{4,8},{8,12},{12,16},{16,20},{20,24},{24,28},{1,5},{5,9},{9,... | collective-permute-start | bytes 24584 | tf_op jit(solution)/shard_map/ppermute | solution.py:19
  137.4 32.2 %collective-permute-start.47 = (f32[2,8,8,1]{1,3,2,0:T(1,128)}, f32[2,8,8,1]{1,3,2,0:T(1,128)}, u32[]{:S(2)}, u32[]{:S(2)}) collective-permute-start(f32[2,8,8,1]{1,3,2,0:T(1,128)} %get-tuple-element.24), channel_id=1, source_target_pairs={{1,0},{2,1},{3,2},{0,3},{5,4},{6,5},{7,6},{4,7},{9,8},{10,9},{11,1... | collective-permute-start | bytes 1544 | tf_op jit(solution)/shard_map/ppermute | solution.py:22
  143.5 28.0 %collective-permute-start.46 = (f32[2,8,8,1]{1,3,2,0:T(1,128)}, f32[2,8,8,1]{1,3,2,0:T(1,128)}, u32[]{:S(2)}, u32[]{:S(2)}) collective-permute-start(f32[2,8,8,1]{1,3,2,0:T(1,128)} %get-tuple-element.23), channel_id=1, source_target_pairs={{0,1},{1,2},{2,3},{3,0},{4,5},{5,6},{6,7},{7,4},{8,9},{9,10},{10,1... | collective-permute-start | bytes 1544 | tf_op jit(solution)/shard_map/ppermute | solution.py:19
  146.8 26.0 %collective-permute-start.45 = (f32[2,8,1,32]{1,3,2,0:T(8,128)}, f32[2,8,1,32]{1,3,2,0:T(8,128)}, u32[]{:S(2)}, u32[]{:S(2)}) collective-permute-start(f32[2,8,1,32]{1,3,2,0:T(8,128)} %get-tuple-element.22), channel_id=1, source_target_pairs={{4,0},{8,4},{12,8},{16,12},{20,16},{24,20},{28,24},{5,1},{9,5},{13... | collective-permute-start | bytes 6152 | tf_op jit(solution)/shard_map/ppermute | solution.py:22
  149.5 32.7 %collective-permute-start.44 = (f32[2,8,1,32]{1,3,2,0:T(8,128)}, f32[2,8,1,32]{1,3,2,0:T(8,128)S(1)}, u32[]{:S(2)}, u32[]{:S(2)}) collective-permute-start(f32[2,8,1,32]{1,3,2,0:T(8,128)} %get-tuple-element.21), channel_id=1, source_target_pairs={{0,4},{4,8},{8,12},{12,16},{16,20},{20,24},{24,28},{1,5},{5,9},{9,... | collective-permute-start | bytes 6152 | tf_op jit(solution)/shard_map/ppermute | solution.py:19
  158.9 37.2 %collective-permute-start.27 = (f32[2,8,16,1]{3,2,1,0:T(8,128)}, f32[2,8,16,1]{3,2,1,0:T(8,128)}, u32[]{:S(2)}, u32[]{:S(2)}) collective-permute-start(f32[2,8,16,1]{3,2,1,0:T(8,128)} %get-tuple-element.44), channel_id=1, source_target_pairs={{1,0},{2,1},{3,2},{0,3},{5,4},{6,5},{7,6},{4,7},{9,8},{10,9},{11,1... | collective-permute-start | bytes 3080 | tf_op jit(solution)/shard_map/ppermute | solution.py:22
  169.6 28.4 %collective-permute-start.26 = (f32[2,8,16,1]{3,2,1,0:T(8,128)}, f32[2,8,16,1]{3,2,1,0:T(8,128)}, u32[]{:S(2)}, u32[]{:S(2)}) collective-permute-start(f32[2,8,16,1]{3,2,1,0:T(8,128)} %get-tuple-element.43), channel_id=1, source_target_pairs={{0,1},{1,2},{2,3},{3,0},{4,5},{5,6},{6,7},{7,4},{8,9},{9,10},{10,1... | collective-permute-start | bytes 3080 | tf_op jit(solution)/shard_map/ppermute | solution.py:19
  171.5 27.8 %collective-permute-start.25 = (f32[2,8,1,64]{3,2,1,0:T(1,128)}, f32[2,8,1,64]{3,2,1,0:T(1,128)S(1)}, u32[]{:S(2)}, u32[]{:S(2)}) collective-permute-start(f32[2,8,1,64]{3,2,1,0:T(1,128)} %get-tuple-element.42), channel_id=1, source_target_pairs={{4,0},{8,4},{12,8},{16,12},{20,16},{24,20},{28,24},{5,1},{9,5},{13... | collective-permute-start | bytes 12296 | tf_op jit(solution)/shard_map/ppermute | solution.py:22
  172.8 34.8 %collective-permute-start.24 = (f32[2,8,1,64]{3,2,1,0:T(1,128)}, f32[2,8,1,64]{3,2,1,0:T(1,128)}, u32[]{:S(2)}, u32[]{:S(2)}) collective-permute-start(f32[2,8,1,64]{3,2,1,0:T(1,128)} %get-tuple-element.41), channel_id=1, source_target_pairs={{0,4},{4,8},{8,12},{12,16},{16,20},{20,24},{24,28},{1,5},{5,9},{9,... | collective-permute-start | bytes 12296 | tf_op jit(solution)/shard_map/ppermute | solution.py:19
  187.8 24.6 %collective-permute-start.7 = (f32[2,8,32,1]{2,1,3,0:T(8,128)}, f32[2,8,32,1]{2,1,3,0:T(8,128)S(1)}, u32[]{:S(2)}, u32[]{:S(2)}) collective-permute-start(f32[2,8,32,1]{2,1,3,0:T(8,128)} %get-tuple-element.16), channel_id=1, source_target_pairs={{1,0},{2,1},{3,2},{0,3},{5,4},{6,5},{7,6},{4,7},{9,8},{10,9},{11,1... | collective-permute-start | bytes 6152 | tf_op jit(solution)/shard_map/ppermute | solution.py:22
  216.8 32.0 %collective-permute-start.11 = (f32[2,8,32,1]{2,1,3,0:T(8,128)}, f32[2,8,32,1]{2,1,3,0:T(8,128)S(1)}, u32[]{:S(2)}, u32[]{:S(2)}) collective-permute-start(f32[2,8,32,1]{2,1,3,0:T(8,128)} %get-tuple-element.12), channel_id=1, source_target_pairs={{1,0},{2,1},{3,2},{0,3},{5,4},{6,5},{7,6},{4,7},{9,8},{10,9},{11,1... | collective-permute-start | bytes 6152 | tf_op jit(solution)/shard_map/ppermute | solution.py:22
  222.0 36.3 %collective-permute-start.10 = (f32[2,8,32,1]{2,1,3,0:T(8,128)}, f32[2,8,32,1]{2,1,3,0:T(8,128)}, u32[]{:S(2)}, u32[]{:S(2)}) collective-permute-start(f32[2,8,32,1]{2,1,3,0:T(8,128)} %get-tuple-element.11), channel_id=1, source_target_pairs={{0,1},{1,2},{2,3},{3,0},{4,5},{5,6},{6,7},{7,4},{8,9},{9,10},{10,1... | collective-permute-start | bytes 6152 | tf_op jit(solution)/shard_map/ppermute | solution.py:19
  228.3 17.9 %collective-permute-start.8 = (f32[2,8,1,128]{3,1,2,0:T(8,128)}, f32[2,8,1,128]{3,1,2,0:T(8,128)S(1)}, u32[]{:S(2)}, u32[]{:S(2)}) collective-permute-start(f32[2,8,1,128]{3,1,2,0:T(8,128)} %copy.356), channel_id=1, source_target_pairs={{0,4},{4,8},{8,12},{12,16},{16,20},{20,24},{24,28},{1,5},{5,9},{9,... | collective-permute-start | bytes 24584 | tf_op jit(solution)/shard_map/ppermute | solution.py:19
  237.7 33.2 %collective-permute-start.31 = (f32[2,8,16,1]{3,2,1,0:T(8,128)}, f32[2,8,16,1]{3,2,1,0:T(8,128)}, u32[]{:S(2)}, u32[]{:S(2)}) collective-permute-start(f32[2,8,16,1]{3,2,1,0:T(8,128)} %get-tuple-element.40), channel_id=1, source_target_pairs={{1,0},{2,1},{3,2},{0,3},{5,4},{6,5},{7,6},{4,7},{9,8},{10,9},{11,1... | collective-permute-start | bytes 3080 | tf_op jit(solution)/shard_map/ppermute | solution.py:22
  242.9 30.0 %collective-permute-start.30 = (f32[2,8,16,1]{3,2,1,0:T(8,128)S(1)}, f32[2,8,16,1]{3,2,1,0:T(8,128)}, u32[]{:S(2)}, u32[]{:S(2)}) collective-permute-start(f32[2,8,16,1]{3,2,1,0:T(8,128)S(1)} %get-tuple-element.39), channel_id=1, source_target_pairs={{0,1},{1,2},{2,3},{3,0},{4,5},{5,6},{6,7},{7,4},{8,9},{9,10},{10,1... | collective-permute-start | bytes 3080 | tf_op jit(solution)/shard_map/ppermute | solution.py:19
  246.2 27.9 %collective-permute-start.29 = (f32[2,8,1,64]{3,2,1,0:T(1,128)}, f32[2,8,1,64]{3,2,1,0:T(1,128)S(1)}, u32[]{:S(2)}, u32[]{:S(2)}) collective-permute-start(f32[2,8,1,64]{3,2,1,0:T(1,128)} %get-tuple-element.38), channel_id=1, source_target_pairs={{4,0},{8,4},{12,8},{16,12},{20,16},{24,20},{28,24},{5,1},{9,5},{13... | collective-permute-start | bytes 12296 | tf_op jit(solution)/shard_map/ppermute | solution.py:22
  248.9 34.1 %collective-permute-start.28 = (f32[2,8,1,64]{3,2,1,0:T(1,128)}, f32[2,8,1,64]{3,2,1,0:T(1,128)}, u32[]{:S(2)}, u32[]{:S(2)}) collective-permute-start(f32[2,8,1,64]{3,2,1,0:T(1,128)} %get-tuple-element.37), channel_id=1, source_target_pairs={{0,4},{4,8},{8,12},{12,16},{16,20},{20,24},{24,28},{1,5},{5,9},{9,... | collective-permute-start | bytes 12296 | tf_op jit(solution)/shard_map/ppermute | solution.py:19
  262.7 25.8 %collective-permute-start.15 = (f32[2,8,32,1]{2,1,3,0:T(8,128)}, f32[2,8,32,1]{2,1,3,0:T(8,128)S(1)}, u32[]{:S(2)}, u32[]{:S(2)}) collective-permute-start(f32[2,8,32,1]{2,1,3,0:T(8,128)} %get-tuple-element.8), channel_id=1, source_target_pairs={{1,0},{2,1},{3,2},{0,3},{5,4},{6,5},{7,6},{4,7},{9,8},{10,9},{11,1... | collective-permute-start | bytes 6152 | tf_op jit(solution)/shard_map/ppermute | solution.py:22
  270.9 17.5 %collective-permute-start.14 = (f32[2,8,32,1]{2,1,3,0:T(8,128)}, f32[2,8,32,1]{2,1,3,0:T(8,128)}, u32[]{:S(2)}, u32[]{:S(2)}) collective-permute-start(f32[2,8,32,1]{2,1,3,0:T(8,128)} %get-tuple-element.7), channel_id=1, source_target_pairs={{0,1},{1,2},{2,3},{3,0},{4,5},{5,6},{6,7},{7,4},{8,9},{9,10},{10,1... | collective-permute-start | bytes 6152 | tf_op jit(solution)/shard_map/ppermute | solution.py:19
  (25 other events, 343.9 us)
Sparse Core Ops, SparseCore 0:
  294.8 131.5 all-reduce.1
where the time goes:
time: 437 us; the launch traced here: 435 us
  starting transfers between devices  205 us (47%)
  waiting for transfers between devices  132 us (30%)
  local copies, waits for them, and re-layouts  54.8 us (13%)
  other arithmetic  29 us (7%)
  between operations  14.2 us (3%)
    psum x1, waiting for transfers between devices, body(): summed = lax.psum(partial_value, 'mem')  132 us
    ppermute x24, starting transfers between devices, with_halo(): lax.ppermute(lax.slice_in_dim(block, block.shape[dim] - width, None, axis...  130 us
    ppermute x24, starting transfers between devices, with_halo(): lax.ppermute(lax.slice_in_dim(block, 0, width, axis=dim), axis, backward)  74.5 us
    slice x28, local copies, waits for them, and re-layouts, with_halo(): lax.slice_in_dim(block, block.shape[dim] - width, None, axis=dim)  19.6 us
    div x11, other arithmetic, diffuse_single(): smoothed = (source + stiffness * beside_all) / (1.0 + 4.0 * stiffness)  14.9 us
    reduce_sum x2, other arithmetic, coarsen(): return jnp.mean(blocks, axis=(-3, -1))  9.21 us
  transfers between devices with their start and end apart: 49, of which 1 were waited for; matrix products, arithmetic and copies ran while one was open for 13% of the time, Pallas kernels for 0%

commit v1 on v0

--- a/solution.py
+++ b/solution.py
@@ -61,7 +61,9 @@
         running = running + weight * member_field * refine(coarse, factor)
     partial_value = jnp.sum(running, axis=0)
     member_count = members.shape[0] * lax.axis_size("mem")
-    summed = lax.psum(partial_value, "mem")
+    summed = partial_value
+    for hop in (1, 2, 4, 8):
+        summed = summed + lax.ppermute(summed, "mem", [(dev, dev ^ hop) for dev in range(16)])
     return summed / (member_count - 1)
 
 

time: 437 us -> 384 us (0.88); the launches traced: 435 us -> 376 us
  waiting for transfers between devices: 132 us -> 59 us
  starting transfers between devices: 205 us -> 236 us
  between operations: 14.2 us -> 0.91 us
    psum x1 -> x0, waiting for transfers between devices: 132 us -> none  [body(): summed = lax.psum(partial_value, 'mem')]
    ppermute x0 -> x4, waiting for transfers between devices: none -> 58.9 us  [body(): lax.ppermute(summed, 'mem', [(dev, dev ^ hop) for dev in range(16)])]
    ppermute x0 -> x4, starting transfers between devices: none -> 31 us  [body(): lax.ppermute(summed, 'mem', [(dev, dev ^ hop) for dev in range(16)])]
  transfers between devices with their start and end apart: 49 -> 52, of which waited for: 1 -> 4; matrix products, arithmetic and copies ran while one was open for 13% -> 15% of each run, Pallas kernels for 0% -> 0%
where the time goes in v1:
time: 384 us; the launch traced here: 376 us
  starting transfers between devices  236 us (61%)
  waiting for transfers between devices  59 us (15%)
  local copies, waits for them, and re-layouts  53.6 us (14%)
  other arithmetic  27 us (7%)
    ppermute x24, starting transfers between devices, with_halo(): lax.ppermute(lax.slice_in_dim(block, block.shape[dim] - width, None, axis...  130 us
    ppermute x24, starting transfers between devices, with_halo(): lax.ppermute(lax.slice_in_dim(block, 0, width, axis=dim), axis, backward)  74.5 us
    ppermute x4, waiting for transfers between devices, body(): lax.ppermute(summed, 'mem', [(dev, dev ^ hop) for dev in range(16)])  58.9 us
    ppermute x4, starting transfers between devices, body(): lax.ppermute(summed, 'mem', [(dev, dev ^ hop) for dev in range(16)])  31 us
    slice x28, local copies, waits for them, and re-layouts, with_halo(): lax.slice_in_dim(block, block.shape[dim] - width, None, axis=dim)  19.5 us
    div x11, other arithmetic, diffuse_single(): smoothed = (source + stiffness * beside_all) / (1.0 + 4.0 * stiffness)  15 us
    reduce_sum x2, other arithmetic, coarsen(): return jnp.mean(blocks, axis=(-3, -1))  9.21 us
    slice x4, local copies, waits for them, and re-layouts, with_halo(): lax.slice_in_dim(block, 0, width, axis=dim)  8.6 us
  transfers between devices with their start and end apart: 52, of which 4 were waited for; matrix products, arithmetic and copies ran while one was open for 15% of the time, Pallas kernels for 0%

profile of v1, /device:TPU:1, one launch (start us, length us, event | category | flops | bytes accessed | tf_op | source)
XLA Modules:
  0.0 376.3 jit_solution(9936508689801043121)
XLA Ops:
  2.4 4.3 %copy.364 = f32[2,8,32,128]{1,3,2,0:T(8,128)} copy(f32[2,8,32,128]{2,1,3,0:T(8,128)S(1)} %convert_multiply_fusion.2) | data formatting | bytes 524288 | tf_op jit(solution)/shard_map/mul | solution.py:56
  6.8 5.6 %reduce_sum.27 = f32[2,8,16,64]{1,3,2,0:T(8,128)S(1)} reduce(f32[2,8,16,2,64,2]{1,5,4,3,2,0:T(2,128)} %bitcast.6, f32[]{:T(128)} %constant.30.clone.1), dimensions={3,5}, to_apply=%region_0.0 | reduce | flops 49152 | bytes 327684 | tf_op jit(solution)/shard_map/reduce_sum | solution.py:34
  13.6 8.4 %collective-permute-start.19 = (f32[2,8,16,1]{3,2,1,0:T(8,128)}, f32[2,8,16,1]{3,2,1,0:T(8,128)}, u32[]{:S(2)}, u32[]{:S(2)}) collective-permute-start(f32[2,8,16,1]{3,2,1,0:T(8,128)} %get-tuple-element.52), channel_id=1, source_target_pairs={{1,0},{2,1},{3,2},{0,3},{5,4},{6,5},{7,6},{4,7},{9,8},{10,9},{11,1... | collective-permute-start | bytes 3080 | tf_op jit(solution)/shard_map/ppermute | solution.py:22
  22.0 3.6 reduce_sum.28
  32.2 8.6 %collective-permute-start.32 = (f32[2,8,1,32]{1,3,2,0:T(8,128)S(1)}, f32[2,8,1,32]{1,3,2,0:T(8,128)S(1)}, u32[]{:S(2)}, u32[]{:S(2)}) collective-permute-start(f32[2,8,1,32]{1,3,2,0:T(8,128)S(1)} %get-tuple-element.33), channel_id=1, source_target_pairs={{0,4},{4,8},{8,12},{12,16},{16,20},{20,24},{24,28},{1,5},{5,9},{9,... | collective-permute-start | bytes 6152 | tf_op jit(solution)/shard_map/ppermute | solution.py:19
  45.1 4.0 %collective-permute-start.39 = (f32[2,8,8,1]{1,3,2,0:T(1,128)}, f32[2,8,8,1]{1,3,2,0:T(1,128)S(1)}, u32[]{:S(2)}, u32[]{:S(2)}) collective-permute-start(f32[2,8,8,1]{1,3,2,0:T(1,128)} %get-tuple-element.32), channel_id=1, source_target_pairs={{1,0},{2,1},{3,2},{0,3},{5,4},{6,5},{7,6},{4,7},{9,8},{10,9},{11,1... | collective-permute-start | bytes 1544 | tf_op jit(solution)/shard_map/ppermute | solution.py:22
  52.3 9.4 %collective-permute-start.36 = (f32[2,8,1,32]{1,3,2,0:T(8,128)}, f32[2,8,1,32]{1,3,2,0:T(8,128)}, u32[]{:S(2)}, u32[]{:S(2)}) collective-permute-start(f32[2,8,1,32]{1,3,2,0:T(8,128)} %get-tuple-element.29), channel_id=1, source_target_pairs={{0,4},{4,8},{8,12},{12,16},{16,20},{20,24},{24,28},{1,5},{5,9},{9,... | collective-permute-start | bytes 6152 | tf_op jit(solution)/shard_map/ppermute | solution.py:19
  68.1 8.2 %collective-permute-start.16 = (f32[2,8,1,64]{3,2,1,0:T(1,128)}, f32[2,8,1,64]{3,2,1,0:T(1,128)S(1)}, u32[]{:S(2)}, u32[]{:S(2)}) collective-permute-start(f32[2,8,1,64]{3,2,1,0:T(1,128)} %get-tuple-element.49), channel_id=1, source_target_pairs={{0,4},{4,8},{8,12},{12,16},{16,20},{20,24},{24,28},{1,5},{5,9},{9,... | collective-permute-start | bytes 12296 | tf_op jit(solution)/shard_map/ppermute | solution.py:19
  76.3 5.2 %collective-permute-start.3 = (f32[2,8,32,1]{2,1,3,0:T(8,128)}, f32[2,8,32,1]{2,1,3,0:T(8,128)S(1)}, u32[]{:S(2)}, u32[]{:S(2)}) collective-permute-start(f32[2,8,32,1]{2,1,3,0:T(8,128)} %get-tuple-element.20), channel_id=1, source_target_pairs={{1,0},{2,1},{3,2},{0,3},{5,4},{6,5},{7,6},{4,7},{9,8},{10,9},{11,1... | collective-permute-start | bytes 6152 | tf_op jit(solution)/shard_map/ppermute | solution.py:22
  84.7 3.4 collective-permute-start.43
  91.3 8.8 %collective-permute-start.40 = (f32[2,8,1,32]{1,3,2,0:T(8,128)S(1)}, f32[2,8,1,32]{1,3,2,0:T(8,128)S(1)}, u32[]{:S(2)}, u32[]{:S(2)}) collective-permute-start(f32[2,8,1,32]{1,3,2,0:T(8,128)S(1)} %get-tuple-element.25), channel_id=1, source_target_pairs={{0,4},{4,8},{8,12},{12,16},{16,20},{20,24},{24,28},{1,5},{5,9},{9,... | collective-permute-start | bytes 6152 | tf_op jit(solution)/shard_map/ppermute | solution.py:19
  100.1 5.2 %collective-permute-start.23 = (f32[2,8,16,1]{3,2,1,0:T(8,128)S(1)}, f32[2,8,16,1]{3,2,1,0:T(8,128)S(1)}, u32[]{:S(2)}, u32[]{:S(2)}) collective-permute-start(f32[2,8,16,1]{3,2,1,0:T(8,128)S(1)} %get-tuple-element.48), channel_id=1, source_target_pairs={{1,0},{2,1},{3,2},{0,3},{5,4},{6,5},{7,6},{4,7},{9,8},{10,9},{11,1... | collective-permute-start | bytes 3080 | tf_op jit(solution)/shard_map/ppermute | solution.py:22
  108.6 8.8 %collective-permute-start.20 = (f32[2,8,1,64]{3,2,1,0:T(1,128)S(1)}, f32[2,8,1,64]{3,2,1,0:T(1,128)S(1)}, u32[]{:S(2)}, u32[]{:S(2)}) collective-permute-start(f32[2,8,1,64]{3,2,1,0:T(1,128)S(1)} %get-tuple-element.45), channel_id=1, source_target_pairs={{0,4},{4,8},{8,12},{12,16},{16,20},{20,24},{24,28},{1,5},{5,9},{9,... | collective-permute-start | bytes 12296 | tf_op jit(solution)/shard_map/ppermute | solution.py:19
  122.0 8.8 %collective-permute-start = (f32[2,8,1,128]{3,1,2,0:T(8,128)S(1)}, f32[2,8,1,128]{3,1,2,0:T(8,128)S(1)}, u32[]{:S(2)}, u32[]{:S(2)}) collective-permute-start(f32[2,8,1,128]{3,1,2,0:T(8,128)S(1)} %copy.348), channel_id=1, source_target_pairs={{0,4},{4,8},{8,12},{12,16},{16,20},{20,24},{24,28},{1,5},{5,9},{9,... | collective-permute-start | bytes 24584 | tf_op jit(solution)/shard_map/ppermute | solution.py:19
  130.9 5.2 %collective-permute-start.47 = (f32[2,8,8,1]{1,3,2,0:T(1,128)}, f32[2,8,8,1]{1,3,2,0:T(1,128)}, u32[]{:S(2)}, u32[]{:S(2)}) collective-permute-start(f32[2,8,8,1]{1,3,2,0:T(1,128)} %get-tuple-element.24), channel_id=1, source_target_pairs={{1,0},{2,1},{3,2},{0,3},{5,4},{6,5},{7,6},{4,7},{9,8},{10,9},{11,1... | collective-permute-start | bytes 1544 | tf_op jit(solution)/shard_map/ppermute | solution.py:22
  143.0 8.8 %collective-permute-start.44 = (f32[2,8,1,32]{1,3,2,0:T(8,128)}, f32[2,8,1,32]{1,3,2,0:T(8,128)S(1)}, u32[]{:S(2)}, u32[]{:S(2)}) collective-permute-start(f32[2,8,1,32]{1,3,2,0:T(8,128)} %get-tuple-element.21), channel_id=1, source_target_pairs={{0,4},{4,8},{8,12},{12,16},{16,20},{20,24},{24,28},{1,5},{5,9},{9,... | collective-permute-start | bytes 6152 | tf_op jit(solution)/shard_map/ppermute | solution.py:19
  152.4 5.3 %collective-permute-start.27 = (f32[2,8,16,1]{3,2,1,0:T(8,128)}, f32[2,8,16,1]{3,2,1,0:T(8,128)}, u32[]{:S(2)}, u32[]{:S(2)}) collective-permute-start(f32[2,8,16,1]{3,2,1,0:T(8,128)} %get-tuple-element.44), channel_id=1, source_target_pairs={{1,0},{2,1},{3,2},{0,3},{5,4},{6,5},{7,6},{4,7},{9,8},{10,9},{11,1... | collective-permute-start | bytes 3080 | tf_op jit(solution)/shard_map/ppermute | solution.py:22
  166.2 9.4 %collective-permute-start.24 = (f32[2,8,1,64]{3,2,1,0:T(1,128)}, f32[2,8,1,64]{3,2,1,0:T(1,128)}, u32[]{:S(2)}, u32[]{:S(2)}) collective-permute-start(f32[2,8,1,64]{3,2,1,0:T(1,128)} %get-tuple-element.41), channel_id=1, source_target_pairs={{0,4},{4,8},{8,12},{12,16},{16,20},{20,24},{24,28},{1,5},{5,9},{9,... | collective-permute-start | bytes 12296 | tf_op jit(solution)/shard_map/ppermute | solution.py:19
  181.3 5.1 %collective-permute-start.7 = (f32[2,8,32,1]{2,1,3,0:T(8,128)}, f32[2,8,32,1]{2,1,3,0:T(8,128)S(1)}, u32[]{:S(2)}, u32[]{:S(2)}) collective-permute-start(f32[2,8,32,1]{2,1,3,0:T(8,128)} %get-tuple-element.16), channel_id=1, source_target_pairs={{1,0},{2,1},{3,2},{0,3},{5,4},{6,5},{7,6},{4,7},{9,8},{10,9},{11,1... | collective-permute-start | bytes 6152 | tf_op jit(solution)/shard_map/ppermute | solution.py:22
  192.8 8.2 %collective-permute-start.4 = (f32[2,8,1,128]{3,1,2,0:T(8,128)}, f32[2,8,1,128]{3,1,2,0:T(8,128)S(1)}, u32[]{:S(2)}, u32[]{:S(2)}) collective-permute-start(f32[2,8,1,128]{3,1,2,0:T(8,128)} %copy.352), channel_id=1, source_target_pairs={{0,4},{4,8},{8,12},{12,16},{16,20},{20,24},{24,28},{1,5},{5,9},{9,... | collective-permute-start | bytes 24584 | tf_op jit(solution)/shard_map/ppermute | solution.py:19
  210.3 5.1 %collective-permute-start.11 = (f32[2,8,32,1]{2,1,3,0:T(8,128)}, f32[2,8,32,1]{2,1,3,0:T(8,128)S(1)}, u32[]{:S(2)}, u32[]{:S(2)}) collective-permute-start(f32[2,8,32,1]{2,1,3,0:T(8,128)} %get-tuple-element.12), channel_id=1, source_target_pairs={{1,0},{2,1},{3,2},{0,3},{5,4},{6,5},{7,6},{4,7},{9,8},{10,9},{11,1... | collective-permute-start | bytes 6152 | tf_op jit(solution)/shard_map/ppermute | solution.py:22
  221.7 8.8 %collective-permute-start.8 = (f32[2,8,1,128]{3,1,2,0:T(8,128)}, f32[2,8,1,128]{3,1,2,0:T(8,128)S(1)}, u32[]{:S(2)}, u32[]{:S(2)}) collective-permute-start(f32[2,8,1,128]{3,1,2,0:T(8,128)} %copy.356), channel_id=1, source_target_pairs={{0,4},{4,8},{8,12},{12,16},{16,20},{20,24},{24,28},{1,5},{5,9},{9,... | collective-permute-start | bytes 24584 | tf_op jit(solution)/shard_map/ppermute | solution.py:19
  231.1 5.1 %collective-permute-start.31 = (f32[2,8,16,1]{3,2,1,0:T(8,128)}, f32[2,8,16,1]{3,2,1,0:T(8,128)}, u32[]{:S(2)}, u32[]{:S(2)}) collective-permute-start(f32[2,8,16,1]{3,2,1,0:T(8,128)} %get-tuple-element.40), channel_id=1, source_target_pairs={{1,0},{2,1},{3,2},{0,3},{5,4},{6,5},{7,6},{4,7},{9,8},{10,9},{11,1... | collective-permute-start | bytes 3080 | tf_op jit(solution)/shard_map/ppermute | solution.py:22
  242.3 9.4 %collective-permute-start.28 = (f32[2,8,1,64]{3,2,1,0:T(1,128)}, f32[2,8,1,64]{3,2,1,0:T(1,128)}, u32[]{:S(2)}, u32[]{:S(2)}) collective-permute-start(f32[2,8,1,64]{3,2,1,0:T(1,128)} %get-tuple-element.37), channel_id=1, source_target_pairs={{0,4},{4,8},{8,12},{12,16},{16,20},{20,24},{24,28},{1,5},{5,9},{9,... | collective-permute-start | bytes 12296 | tf_op jit(solution)/shard_map/ppermute | solution.py:19
  256.0 5.1 %collective-permute-start.15 = (f32[2,8,32,1]{2,1,3,0:T(8,128)}, f32[2,8,32,1]{2,1,3,0:T(8,128)S(1)}, u32[]{:S(2)}, u32[]{:S(2)}) collective-permute-start(f32[2,8,32,1]{2,1,3,0:T(8,128)} %get-tuple-element.8), channel_id=1, source_target_pairs={{1,0},{2,1},{3,2},{0,3},{5,4},{6,5},{7,6},{4,7},{9,8},{10,9},{11,1... | collective-permute-start | bytes 6152 | tf_op jit(solution)/shard_map/ppermute | solution.py:22
  267.5 8.8 %collective-permute-start.12 = (f32[2,8,1,128]{3,1,2,0:T(8,128)}, f32[2,8,1,128]{3,1,2,0:T(8,128)}, u32[]{:S(2)}, u32[]{:S(2)}) collective-permute-start(f32[2,8,1,128]{3,1,2,0:T(8,128)} %copy.360), channel_id=1, source_target_pairs={{0,4},{4,8},{8,12},{12,16},{16,20},{20,24},{24,28},{1,5},{5,9},{9,... | collective-permute-start | bytes 24584 | tf_op jit(solution)/shard_map/ppermute | solution.py:19
  285.4 15.2 %collective-permute-start.48 = (f32[8,32,128]{1,0,2:T(8,128)S(1)}, f32[8,32,128]{1,0,2:T(8,128)S(1)}, u32[]{:S(2)}, u32[]{:S(2)}) collective-permute-start(f32[8,32,128]{1,0,2:T(8,128)S(1)} %fusion.3), channel_id=1, source_target_pairs={{0,32},{32,0},{64,96},{96,64},{128,160},{160,128},{192,224},{224,1... | collective-permute-start | bytes 393224 | tf_op jit(solution)/shard_map/ppermute | solution.py:66
  305.4 11.8 %collective-permute-done.49 = f32[8,32,128]{1,0,2:T(8,128)S(1)} collective-permute-done((f32[8,32,128]{1,0,2:T(8,128)S(1)}, f32[8,32,128]{1,0,2:T(8,128)S(1)}, u32[]{:S(2)}, u32[]{:S(2)}) %collective-permute-start.49) | collective-permute-done | bytes 131104 | tf_op jit(solution)/shard_map/ppermute | solution.py:66
  317.2 4.2 %collective-permute-start.50 = (f32[8,32,128]{1,0,2:T(8,128)S(1)}, f32[8,32,128]{1,0,2:T(8,128)S(1)}, u32[]{:S(2)}, u32[]{:S(2)}) collective-permute-start(f32[8,32,128]{1,0,2:T(8,128)S(1)} %add.213), channel_id=1, source_target_pairs={{0,128},{32,160},{64,192},{96,224},{128,0},{160,32},{192,64},{224,... | collective-permute-start | bytes 393224 | tf_op jit(solution)/shard_map/ppermute | solution.py:66
  321.4 22.6 %collective-permute-done.50 = f32[8,32,128]{1,0,2:T(8,128)S(1)} collective-permute-done((f32[8,32,128]{1,0,2:T(8,128)S(1)}, f32[8,32,128]{1,0,2:T(8,128)S(1)}, u32[]{:S(2)}, u32[]{:S(2)}) %collective-permute-start.50) | collective-permute-done | bytes 131104 | tf_op jit(solution)/shard_map/ppermute | solution.py:66
  344.1 8.4 %collective-permute-start.51 = (f32[8,32,128]{1,0,2:T(8,128)S(1)}, f32[8,32,128]{1,0,2:T(8,128)S(1)}, u32[]{:S(2)}, u32[]{:S(2)}) collective-permute-start(f32[8,32,128]{1,0,2:T(8,128)S(1)} %add.214), channel_id=1, source_target_pairs={{0,256},{32,288},{64,320},{96,352},{128,384},{160,416},{192,448},{... | collective-permute-start | bytes 393224 | tf_op jit(solution)/shard_map/ppermute | solution.py:66
  352.5 22.9 %collective-permute-done.51 = f32[8,32,128]{1,0,2:T(8,128)S(1)} collective-permute-done((f32[8,32,128]{1,0,2:T(8,128)S(1)}, f32[8,32,128]{1,0,2:T(8,128)S(1)}, u32[]{:S(2)}, u32[]{:S(2)}) %collective-permute-start.51) | collective-permute-done | bytes 131104 | tf_op jit(solution)/shard_map/ppermute | solution.py:66
  (162 shorter events, 113.7 us)
Async XLA Ops:
  13.6 69.4 %collective-permute-start.19 = (f32[2,8,16,1]{3,2,1,0:T(8,128)}, f32[2,8,16,1]{3,2,1,0:T(8,128)}, u32[]{:S(2)}, u32[]{:S(2)}) collective-permute-start(f32[2,8,16,1]{3,2,1,0:T(8,128)} %get-tuple-element.52), channel_id=1, source_target_pairs={{1,0},{2,1},{3,2},{0,3},{5,4},{6,5},{7,6},{4,7},{9,8},{10,9},{11,1... | collective-permute-start | bytes 3080 | tf_op jit(solution)/shard_map/ppermute | solution.py:22
  25.6 18.0 %collective-permute-start.35 = (f32[2,8,8,1]{1,3,2,0:T(1,128)S(1)}, f32[2,8,8,1]{1,3,2,0:T(1,128)S(1)}, u32[]{:S(2)}, u32[]{:S(2)}) collective-permute-start(f32[2,8,8,1]{1,3,2,0:T(1,128)S(1)} %get-tuple-element.36), channel_id=1, source_target_pairs={{1,0},{2,1},{3,2},{0,3},{5,4},{6,5},{7,6},{4,7},{9,8},{10,9},{11,1... | collective-permute-start | bytes 1544 | tf_op jit(solution)/shard_map/ppermute | solution.py:22
  45.1 19.7 %collective-permute-start.39 = (f32[2,8,8,1]{1,3,2,0:T(1,128)}, f32[2,8,8,1]{1,3,2,0:T(1,128)S(1)}, u32[]{:S(2)}, u32[]{:S(2)}) collective-permute-start(f32[2,8,8,1]{1,3,2,0:T(1,128)} %get-tuple-element.32), channel_id=1, source_target_pairs={{1,0},{2,1},{3,2},{0,3},{5,4},{6,5},{7,6},{4,7},{9,8},{10,9},{11,1... | collective-permute-start | bytes 1544 | tf_op jit(solution)/shard_map/ppermute | solution.py:22
  49.1 17.7 %collective-permute-start.38 = (f32[2,8,8,1]{1,3,2,0:T(1,128)}, f32[2,8,8,1]{1,3,2,0:T(1,128)}, u32[]{:S(2)}, u32[]{:S(2)}) collective-permute-start(f32[2,8,8,1]{1,3,2,0:T(1,128)} %get-tuple-element.31), channel_id=1, source_target_pairs={{0,1},{1,2},{2,3},{3,0},{4,5},{5,6},{6,7},{7,4},{8,9},{9,10},{10,1... | collective-permute-start | bytes 1544 | tf_op jit(solution)/shard_map/ppermute | solution.py:19
  52.3 24.0 %collective-permute-start.36 = (f32[2,8,1,32]{1,3,2,0:T(8,128)}, f32[2,8,1,32]{1,3,2,0:T(8,128)}, u32[]{:S(2)}, u32[]{:S(2)}) collective-permute-start(f32[2,8,1,32]{1,3,2,0:T(8,128)} %get-tuple-element.29), channel_id=1, source_target_pairs={{0,4},{4,8},{8,12},{12,16},{16,20},{20,24},{24,28},{1,5},{5,9},{9,... | collective-permute-start | bytes 6152 | tf_op jit(solution)/shard_map/ppermute | solution.py:19
  64.8 18.2 %collective-permute-start.18 = (f32[2,8,16,1]{3,2,1,0:T(8,128)}, f32[2,8,16,1]{3,2,1,0:T(8,128)S(1)}, u32[]{:S(2)}, u32[]{:S(2)}) collective-permute-start(f32[2,8,16,1]{3,2,1,0:T(8,128)} %get-tuple-element.51), channel_id=1, source_target_pairs={{0,1},{1,2},{2,3},{3,0},{4,5},{5,6},{6,7},{7,4},{8,9},{9,10},{10,1... | collective-permute-start | bytes 3080 | tf_op jit(solution)/shard_map/ppermute | solution.py:19
  76.3 66.6 %collective-permute-start.3 = (f32[2,8,32,1]{2,1,3,0:T(8,128)}, f32[2,8,32,1]{2,1,3,0:T(8,128)S(1)}, u32[]{:S(2)}, u32[]{:S(2)}) collective-permute-start(f32[2,8,32,1]{2,1,3,0:T(8,128)} %get-tuple-element.20), channel_id=1, source_target_pairs={{1,0},{2,1},{3,2},{0,3},{5,4},{6,5},{7,6},{4,7},{9,8},{10,9},{11,1... | collective-permute-start | bytes 6152 | tf_op jit(solution)/shard_map/ppermute | solution.py:22
  91.3 17.3 %collective-permute-start.40 = (f32[2,8,1,32]{1,3,2,0:T(8,128)S(1)}, f32[2,8,1,32]{1,3,2,0:T(8,128)S(1)}, u32[]{:S(2)}, u32[]{:S(2)}) collective-permute-start(f32[2,8,1,32]{1,3,2,0:T(8,128)S(1)} %get-tuple-element.25), channel_id=1, source_target_pairs={{0,4},{4,8},{8,12},{12,16},{16,20},{20,24},{24,28},{1,5},{5,9},{9,... | collective-permute-start | bytes 6152 | tf_op jit(solution)/shard_map/ppermute | solution.py:19
  100.1 18.7 %collective-permute-start.23 = (f32[2,8,16,1]{3,2,1,0:T(8,128)S(1)}, f32[2,8,16,1]{3,2,1,0:T(8,128)S(1)}, u32[]{:S(2)}, u32[]{:S(2)}) collective-permute-start(f32[2,8,16,1]{3,2,1,0:T(8,128)S(1)} %get-tuple-element.48), channel_id=1, source_target_pairs={{1,0},{2,1},{3,2},{0,3},{5,4},{6,5},{7,6},{4,7},{9,8},{10,9},{11,1... | collective-permute-start | bytes 3080 | tf_op jit(solution)/shard_map/ppermute | solution.py:22
  108.6 22.3 %collective-permute-start.20 = (f32[2,8,1,64]{3,2,1,0:T(1,128)S(1)}, f32[2,8,1,64]{3,2,1,0:T(1,128)S(1)}, u32[]{:S(2)}, u32[]{:S(2)}) collective-permute-start(f32[2,8,1,64]{3,2,1,0:T(1,128)S(1)} %get-tuple-element.45), channel_id=1, source_target_pairs={{0,4},{4,8},{8,12},{12,16},{16,20},{20,24},{24,28},{1,5},{5,9},{9,... | collective-permute-start | bytes 12296 | tf_op jit(solution)/shard_map/ppermute | solution.py:19
  118.8 32.9 %collective-permute-start.2 = (f32[2,8,32,1]{2,1,3,0:T(8,128)}, f32[2,8,32,1]{2,1,3,0:T(8,128)S(1)}, u32[]{:S(2)}, u32[]{:S(2)}) collective-permute-start(f32[2,8,32,1]{2,1,3,0:T(8,128)} %get-tuple-element.19), channel_id=1, source_target_pairs={{0,1},{1,2},{2,3},{3,0},{4,5},{5,6},{6,7},{7,4},{8,9},{9,10},{10,1... | collective-permute-start | bytes 6152 | tf_op jit(solution)/shard_map/ppermute | solution.py:19
  122.0 18.3 %collective-permute-start = (f32[2,8,1,128]{3,1,2,0:T(8,128)S(1)}, f32[2,8,1,128]{3,1,2,0:T(8,128)S(1)}, u32[]{:S(2)}, u32[]{:S(2)}) collective-permute-start(f32[2,8,1,128]{3,1,2,0:T(8,128)S(1)} %copy.348), channel_id=1, source_target_pairs={{0,4},{4,8},{8,12},{12,16},{16,20},{20,24},{24,28},{1,5},{5,9},{9,... | collective-permute-start | bytes 24584 | tf_op jit(solution)/shard_map/ppermute | solution.py:19
  130.9 32.1 %collective-permute-start.47 = (f32[2,8,8,1]{1,3,2,0:T(1,128)}, f32[2,8,8,1]{1,3,2,0:T(1,128)}, u32[]{:S(2)}, u32[]{:S(2)}) collective-permute-start(f32[2,8,8,1]{1,3,2,0:T(1,128)} %get-tuple-element.24), channel_id=1, source_target_pairs={{1,0},{2,1},{3,2},{0,3},{5,4},{6,5},{7,6},{4,7},{9,8},{10,9},{11,1... | collective-permute-start | bytes 1544 | tf_op jit(solution)/shard_map/ppermute | solution.py:22
  137.0 27.9 %collective-permute-start.46 = (f32[2,8,8,1]{1,3,2,0:T(1,128)}, f32[2,8,8,1]{1,3,2,0:T(1,128)}, u32[]{:S(2)}, u32[]{:S(2)}) collective-permute-start(f32[2,8,8,1]{1,3,2,0:T(1,128)} %get-tuple-element.23), channel_id=1, source_target_pairs={{0,1},{1,2},{2,3},{3,0},{4,5},{5,6},{6,7},{7,4},{8,9},{9,10},{10,1... | collective-permute-start | bytes 1544 | tf_op jit(solution)/shard_map/ppermute | solution.py:19
  140.3 25.9 %collective-permute-start.45 = (f32[2,8,1,32]{1,3,2,0:T(8,128)}, f32[2,8,1,32]{1,3,2,0:T(8,128)}, u32[]{:S(2)}, u32[]{:S(2)}) collective-permute-start(f32[2,8,1,32]{1,3,2,0:T(8,128)} %get-tuple-element.22), channel_id=1, source_target_pairs={{4,0},{8,4},{12,8},{16,12},{20,16},{24,20},{28,24},{5,1},{9,5},{13... | collective-permute-start | bytes 6152 | tf_op jit(solution)/shard_map/ppermute | solution.py:22
  143.0 32.7 %collective-permute-start.44 = (f32[2,8,1,32]{1,3,2,0:T(8,128)}, f32[2,8,1,32]{1,3,2,0:T(8,128)S(1)}, u32[]{:S(2)}, u32[]{:S(2)}) collective-permute-start(f32[2,8,1,32]{1,3,2,0:T(8,128)} %get-tuple-element.21), channel_id=1, source_target_pairs={{0,4},{4,8},{8,12},{12,16},{16,20},{20,24},{24,28},{1,5},{5,9},{9,... | collective-permute-start | bytes 6152 | tf_op jit(solution)/shard_map/ppermute | solution.py:19
  152.4 37.2 %collective-permute-start.27 = (f32[2,8,16,1]{3,2,1,0:T(8,128)}, f32[2,8,16,1]{3,2,1,0:T(8,128)}, u32[]{:S(2)}, u32[]{:S(2)}) collective-permute-start(f32[2,8,16,1]{3,2,1,0:T(8,128)} %get-tuple-element.44), channel_id=1, source_target_pairs={{1,0},{2,1},{3,2},{0,3},{5,4},{6,5},{7,6},{4,7},{9,8},{10,9},{11,1... | collective-permute-start | bytes 3080 | tf_op jit(solution)/shard_map/ppermute | solution.py:22
  163.0 28.5 %collective-permute-start.26 = (f32[2,8,16,1]{3,2,1,0:T(8,128)}, f32[2,8,16,1]{3,2,1,0:T(8,128)}, u32[]{:S(2)}, u32[]{:S(2)}) collective-permute-start(f32[2,8,16,1]{3,2,1,0:T(8,128)} %get-tuple-element.43), channel_id=1, source_target_pairs={{0,1},{1,2},{2,3},{3,0},{4,5},{5,6},{6,7},{7,4},{8,9},{9,10},{10,1... | collective-permute-start | bytes 3080 | tf_op jit(solution)/shard_map/ppermute | solution.py:19
  164.9 27.8 %collective-permute-start.25 = (f32[2,8,1,64]{3,2,1,0:T(1,128)}, f32[2,8,1,64]{3,2,1,0:T(1,128)S(1)}, u32[]{:S(2)}, u32[]{:S(2)}) collective-permute-start(f32[2,8,1,64]{3,2,1,0:T(1,128)} %get-tuple-element.42), channel_id=1, source_target_pairs={{4,0},{8,4},{12,8},{16,12},{20,16},{24,20},{28,24},{5,1},{9,5},{13... | collective-permute-start | bytes 12296 | tf_op jit(solution)/shard_map/ppermute | solution.py:22
  166.2 34.8 %collective-permute-start.24 = (f32[2,8,1,64]{3,2,1,0:T(1,128)}, f32[2,8,1,64]{3,2,1,0:T(1,128)}, u32[]{:S(2)}, u32[]{:S(2)}) collective-permute-start(f32[2,8,1,64]{3,2,1,0:T(1,128)} %get-tuple-element.41), channel_id=1, source_target_pairs={{0,4},{4,8},{8,12},{12,16},{16,20},{20,24},{24,28},{1,5},{5,9},{9,... | collective-permute-start | bytes 12296 | tf_op jit(solution)/shard_map/ppermute | solution.py:19
  181.3 24.6 %collective-permute-start.7 = (f32[2,8,32,1]{2,1,3,0:T(8,128)}, f32[2,8,32,1]{2,1,3,0:T(8,128)S(1)}, u32[]{:S(2)}, u32[]{:S(2)}) collective-permute-start(f32[2,8,32,1]{2,1,3,0:T(8,128)} %get-tuple-element.16), channel_id=1, source_target_pairs={{1,0},{2,1},{3,2},{0,3},{5,4},{6,5},{7,6},{4,7},{9,8},{10,9},{11,1... | collective-permute-start | bytes 6152 | tf_op jit(solution)/shard_map/ppermute | solution.py:22
  210.3 32.0 %collective-permute-start.11 = (f32[2,8,32,1]{2,1,3,0:T(8,128)}, f32[2,8,32,1]{2,1,3,0:T(8,128)S(1)}, u32[]{:S(2)}, u32[]{:S(2)}) collective-permute-start(f32[2,8,32,1]{2,1,3,0:T(8,128)} %get-tuple-element.12), channel_id=1, source_target_pairs={{1,0},{2,1},{3,2},{0,3},{5,4},{6,5},{7,6},{4,7},{9,8},{10,9},{11,1... | collective-permute-start | bytes 6152 | tf_op jit(solution)/shard_map/ppermute | solution.py:22
  215.4 36.2 %collective-permute-start.10 = (f32[2,8,32,1]{2,1,3,0:T(8,128)}, f32[2,8,32,1]{2,1,3,0:T(8,128)}, u32[]{:S(2)}, u32[]{:S(2)}) collective-permute-start(f32[2,8,32,1]{2,1,3,0:T(8,128)} %get-tuple-element.11), channel_id=1, source_target_pairs={{0,1},{1,2},{2,3},{3,0},{4,5},{5,6},{6,7},{7,4},{8,9},{9,10},{10,1... | collective-permute-start | bytes 6152 | tf_op jit(solution)/shard_map/ppermute | solution.py:19
  221.7 17.9 %collective-permute-start.8 = (f32[2,8,1,128]{3,1,2,0:T(8,128)}, f32[2,8,1,128]{3,1,2,0:T(8,128)S(1)}, u32[]{:S(2)}, u32[]{:S(2)}) collective-permute-start(f32[2,8,1,128]{3,1,2,0:T(8,128)} %copy.356), channel_id=1, source_target_pairs={{0,4},{4,8},{8,12},{12,16},{16,20},{20,24},{24,28},{1,5},{5,9},{9,... | collective-permute-start | bytes 24584 | tf_op jit(solution)/shard_map/ppermute | solution.py:19
  231.1 33.2 %collective-permute-start.31 = (f32[2,8,16,1]{3,2,1,0:T(8,128)}, f32[2,8,16,1]{3,2,1,0:T(8,128)}, u32[]{:S(2)}, u32[]{:S(2)}) collective-permute-start(f32[2,8,16,1]{3,2,1,0:T(8,128)} %get-tuple-element.40), channel_id=1, source_target_pairs={{1,0},{2,1},{3,2},{0,3},{5,4},{6,5},{7,6},{4,7},{9,8},{10,9},{11,1... | collective-permute-start | bytes 3080 | tf_op jit(solution)/shard_map/ppermute | solution.py:22
  236.3 29.9 %collective-permute-start.30 = (f32[2,8,16,1]{3,2,1,0:T(8,128)S(1)}, f32[2,8,16,1]{3,2,1,0:T(8,128)}, u32[]{:S(2)}, u32[]{:S(2)}) collective-permute-start(f32[2,8,16,1]{3,2,1,0:T(8,128)S(1)} %get-tuple-element.39), channel_id=1, source_target_pairs={{0,1},{1,2},{2,3},{3,0},{4,5},{5,6},{6,7},{7,4},{8,9},{9,10},{10,1... | collective-permute-start | bytes 3080 | tf_op jit(solution)/shard_map/ppermute | solution.py:19
  239.6 27.9 %collective-permute-start.29 = (f32[2,8,1,64]{3,2,1,0:T(1,128)}, f32[2,8,1,64]{3,2,1,0:T(1,128)S(1)}, u32[]{:S(2)}, u32[]{:S(2)}) collective-permute-start(f32[2,8,1,64]{3,2,1,0:T(1,128)} %get-tuple-element.38), channel_id=1, source_target_pairs={{4,0},{8,4},{12,8},{16,12},{20,16},{24,20},{28,24},{5,1},{9,5},{13... | collective-permute-start | bytes 12296 | tf_op jit(solution)/shard_map/ppermute | solution.py:22
  242.3 34.1 %collective-permute-start.28 = (f32[2,8,1,64]{3,2,1,0:T(1,128)}, f32[2,8,1,64]{3,2,1,0:T(1,128)}, u32[]{:S(2)}, u32[]{:S(2)}) collective-permute-start(f32[2,8,1,64]{3,2,1,0:T(1,128)} %get-tuple-element.37), channel_id=1, source_target_pairs={{0,4},{4,8},{8,12},{12,16},{16,20},{20,24},{24,28},{1,5},{5,9},{9,... | collective-permute-start | bytes 12296 | tf_op jit(solution)/shard_map/ppermute | solution.py:19
  256.0 25.8 %collective-permute-start.15 = (f32[2,8,32,1]{2,1,3,0:T(8,128)}, f32[2,8,32,1]{2,1,3,0:T(8,128)S(1)}, u32[]{:S(2)}, u32[]{:S(2)}) collective-permute-start(f32[2,8,32,1]{2,1,3,0:T(8,128)} %get-tuple-element.8), channel_id=1, source_target_pairs={{1,0},{2,1},{3,2},{0,3},{5,4},{6,5},{7,6},{4,7},{9,8},{10,9},{11,1... | collective-permute-start | bytes 6152 | tf_op jit(solution)/shard_map/ppermute | solution.py:22
  264.3 17.5 %collective-permute-start.14 = (f32[2,8,32,1]{2,1,3,0:T(8,128)}, f32[2,8,32,1]{2,1,3,0:T(8,128)}, u32[]{:S(2)}, u32[]{:S(2)}) collective-permute-start(f32[2,8,32,1]{2,1,3,0:T(8,128)} %get-tuple-element.7), channel_id=1, source_target_pairs={{0,1},{1,2},{2,3},{3,0},{4,5},{5,6},{6,7},{7,4},{8,9},{9,10},{10,1... | collective-permute-start | bytes 6152 | tf_op jit(solution)/shard_map/ppermute | solution.py:19
  317.2 26.9 %collective-permute-start.50 = (f32[8,32,128]{1,0,2:T(8,128)S(1)}, f32[8,32,128]{1,0,2:T(8,128)S(1)}, u32[]{:S(2)}, u32[]{:S(2)}) collective-permute-start(f32[8,32,128]{1,0,2:T(8,128)S(1)} %add.213), channel_id=1, source_target_pairs={{0,128},{32,160},{64,192},{96,224},{128,0},{160,32},{192,64},{224,... | collective-permute-start | bytes 393224 | tf_op jit(solution)/shard_map/ppermute | solution.py:66
  344.1 31.3 %collective-permute-start.51 = (f32[8,32,128]{1,0,2:T(8,128)S(1)}, f32[8,32,128]{1,0,2:T(8,128)S(1)}, u32[]{:S(2)}, u32[]{:S(2)}) collective-permute-start(f32[8,32,128]{1,0,2:T(8,128)S(1)} %add.214), channel_id=1, source_target_pairs={{0,256},{32,288},{64,320},{96,352},{128,384},{160,416},{192,448},{... | collective-permute-start | bytes 393224 | tf_op jit(solution)/shard_map/ppermute | solution.py:66
  (28 other events, 392.7 us)
